TPU v7x, 32 devices: a whole 2x2x4 slice. The times are simulated.
32 devices in a mesh: expert: 8 (over z, x), hidden: 4 (over y, core).
Axes of the slice: x: 2, y: 2, z: 4, core: 2. Of those that a mesh axis runs over, the one named last changes fastest.
Arguments:
- tokens: bfloat16 [1024, 4096], P('expert'), may hold values from -6 to 6
- cotangent: bfloat16 [1024, 4096], P('expert'), may hold values from -3 to 3
- expert_ids: int32 [1024, 2], P('expert'), may hold values from 0 to 7, as said below
- gate_codes: int32 [1024, 2], P('expert'), may hold values from 1 to 256
- up_weight: bfloat16 [8, 4096, 1024], P('expert', None, 'hidden'), may hold values from -0.09375 to 0.09375
- down_weight: bfloat16 [8, 1024, 4096], P('expert', 'hidden'), may hold values from -0.1875 to 0.1875
- threshold_state: int32 [8, 1024], P('expert', 'hidden'), may hold values from -64 to 191
- spike_mask: int32 [8, 1024], P('expert', 'hidden'), may hold values 0 or 1
Outputs:
- layer_out: bfloat16 [1024, 4096], P('expert', 'hidden')
- token_grad: bfloat16 [1024, 4096], P('expert', 'hidden')
- up_grad: bfloat16 [8, 4096, 1024], P('expert', None, 'hidden')
- down_grad: bfloat16 [8, 1024, 4096], P('expert', 'hidden')
Inputs may be any that keep to these rules, and one draw needn't show every extreme that they name: `expert_ids`: in each aligned block of 128 tokens, every expert is named by no slot or by exactly 64 slots; a token's two experts differ; one expert is named by 64 slots in every block.
All inputs are finite; a program needn't handle non-finite values. No bound on the sum of `spike_mask` on one device may be relied on, other than what follows from the above.
Results may differ from a plain program's by a relative error of at most 0.015.
Values may be sent and summed in bfloat16 or wider, within the bound.
A program may use at most 128 MiB of HBM per device.

v0:
```python
import jax
import jax.numpy as jnp
from jax import lax
from jax.sharding import PartitionSpec as P

SHARPNESS = 2.0


def expert_pass(inputs, upstream, slot_gate, up_block, down_block, threshold_row, mask_row):
    pre = jnp.dot(inputs, up_block, preferred_element_type=jnp.float32)
    level = threshold_row.astype(jnp.float32) / 64.0
    opened = mask_row.astype(jnp.float32)
    sigma = jax.nn.sigmoid(SHARPNESS * (pre - level))
    weight_col = slot_gate.astype(jnp.float32)[:, None]
    gated = (weight_col * opened * pre * sigma).astype(jnp.bfloat16)
    back_hidden = (
        jnp.einsum("rd,fd->rf", upstream, down_block, preferred_element_type=jnp.float32)
        * weight_col
    )
    slope = opened * (sigma + SHARPNESS * pre * sigma * (1.0 - sigma))
    dpre = (back_hidden * slope).astype(jnp.bfloat16)
    part_out = jnp.dot(gated, down_block, preferred_element_type=jnp.float32)
    part_back = jnp.einsum("rf,df->rd", dpre, up_block, preferred_element_type=jnp.float32)
    grad_down = jnp.einsum("rf,rd->fd", gated, upstream, preferred_element_type=jnp.float32).astype(
        jnp.bfloat16
    )
    grad_up = jnp.einsum("rd,rf->df", inputs, dpre, preferred_element_type=jnp.float32).astype(
        jnp.bfloat16
    )
    return (part_out, part_back, grad_up, grad_down)


def shards(
    tokens, cotangent, expert_ids, gate_codes, up_weight, down_weight, threshold_state, spike_mask
):
    groups = lax.axis_size("expert")
    tok_rows, width = tokens.shape
    top = expert_ids.shape[1]
    capacity = 4 * tok_rows // groups
    pairs = tok_rows * top
    slots = groups * capacity
    flat_ids = expert_ids.reshape(pairs)
    pair_index = jnp.arange(pairs, dtype=jnp.int32)
    earlier = (flat_ids[None, :] == flat_ids[:, None]) & (pair_index[None, :] < pair_index[:, None])
    place = jnp.sum(earlier.astype(jnp.int32), axis=1)
    target = flat_ids * capacity + place
    slot_index = jnp.arange(slots, dtype=jnp.int32)
    hits = target[None, :] == slot_index[:, None]
    filled = jnp.any(hits, axis=1)
    source_pair = jnp.sum(jnp.where(hits, pair_index[None, :], 0), axis=1)
    source_token = source_pair // top
    gate_values = gate_codes.reshape(pairs).astype(jnp.float32) / 256.0
    slot_gate = (
        jnp.where(filled, gate_values[source_pair], 0.0)
        .astype(jnp.bfloat16)
        .reshape(groups, capacity)
    )
    keep = filled[:, None]
    nothing = jnp.zeros((), jnp.bfloat16)
    send_in = jnp.where(keep, tokens[source_token], nothing).reshape(groups, capacity, width)
    send_up = jnp.where(keep, cotangent[source_token], nothing).reshape(groups, capacity, width)
    got_in, got_up, got_gate = (
        lax.all_to_all(send_in, "expert", split_axis=0, concat_axis=0, tiled=True),
        lax.all_to_all(send_up, "expert", split_axis=0, concat_axis=0, tiled=True),
        lax.all_to_all(slot_gate, "expert", split_axis=0, concat_axis=0, tiled=True),
    )
    part_out, part_back, grad_up, grad_down = expert_pass(
        got_in.reshape(slots, width),
        got_up.reshape(slots, width),
        got_gate.reshape(slots),
        up_weight[0],
        down_weight[0],
        threshold_state[0],
        spike_mask[0],
    )
    rounded_out = part_out.astype(jnp.bfloat16)
    rounded_back = part_back.astype(jnp.bfloat16)
    kept_out, kept_back = lax.optimization_barrier((rounded_out, rounded_back))
    out_sum, back_sum = (
        lax.psum_scatter(
            kept_out.astype(jnp.float32).astype(jnp.bfloat16),
            "hidden",
            scatter_dimension=1,
            tiled=True,
        ).astype(jnp.float32),
        lax.psum_scatter(
            kept_back.astype(jnp.float32).astype(jnp.bfloat16),
            "hidden",
            scatter_dimension=1,
            tiled=True,
        ).astype(jnp.float32),
    )
    share = out_sum.shape[1]
    home_out, home_back = (
        lax.all_to_all(
            out_sum.reshape(groups, capacity, share).astype(jnp.bfloat16),
            "expert",
            split_axis=0,
            concat_axis=0,
            tiled=True,
        ).astype(jnp.float32),
        lax.all_to_all(
            back_sum.reshape(groups, capacity, share).astype(jnp.bfloat16),
            "expert",
            split_axis=0,
            concat_axis=0,
            tiled=True,
        ).astype(jnp.float32),
    )
    layer_out = jnp.sum(
        home_out.reshape(slots, share)[target].reshape(tok_rows, top, share), axis=1
    )
    token_grad = jnp.sum(
        home_back.reshape(slots, share)[target].reshape(tok_rows, top, share), axis=1
    )
    return (
        layer_out.astype(jnp.bfloat16),
        token_grad.astype(jnp.bfloat16),
        grad_up[None],
        grad_down[None],
    )


def solution(mesh):
    placed = (
        P("expert", None),
        P("expert", None),
        P("expert", None),
        P("expert", None),
        P("expert", None, "hidden"),
        P("expert", "hidden", None),
        P("expert", "hidden"),
        P("expert", "hidden"),
    )
    return jax.shard_map(
        shards,
        mesh=mesh,
        in_specs=placed,
        out_specs=(
            P("expert", "hidden"),
            P("expert", "hidden"),
            P("expert", None, "hidden"),
            P("expert", "hidden", None),
        ),
        check_vma=False,
    )
```

profile of v0, /device:TPU:0, one launch (start us, length us, event | category | flops | bytes accessed | tf_op | source)
XLA Modules:
  0.0 387.3 jit_solution(12582803013536145401)
XLA Ops:
  9.8 3.4 gather_fusion
  13.9 7.3 %all-to-all-start = ((bf16[8,1,64]{2,1,0:T(2,128)(2,1)}), bf16[8,1,64]{2,1,0:T(2,128)(2,1)S(1)}, u32[]{:S(2)}, u32[]{:S(2)}) async-start(bf16[8,1,64]{2,1,0:T(2,128)(2,1)} %convert_element_type.98), calls=%async_computation | async-start | bytes 8192 | tf_op jit(solution)/shard_map/all_to_all | solution.py:65
  21.2 4.4 %gather_fusion.2 = bf16[512,4096]{1,0:T(8,128)(2,1)} fusion(bf16[128,4096]{1,0:T(8,128)(2,1)S(1)} %copy-done.1, s32[1024]{0:T(1024)S(1)} %pad_clamp_fusion.1), kind=kCustom, calls=%fused_computation.2 | custom fusion | bytes 8390656 | tf_op jit(solution)/shard_map/gather | solution.py:61
  25.6 9.9 %gather_fusion.1 = bf16[512,4096]{1,0:T(8,128)(2,1)} fusion(bf16[128,4096]{1,0:T(8,128)(2,1)} %param.8, s32[1024]{0:T(1024)S(1)} %pad_clamp_fusion.1), kind=kCustom, calls=%fused_computation.1 | custom fusion | bytes 8390656 | tf_op jit(solution)/shard_map/gather | solution.py:60
  35.5 5.9 %broadcast_select_fusion = (bf16[8,64,4096]{2,1,0:T(8,128)(2,1)}, bf16[8,64,4096]{2,1,0:T(8,128)(2,1)}) fusion(bf16[8,64,4096]{2,1,0:T(8,128)(2,1)} %bitcast.45, pred[8,64]{1,0:T(8,128)(4,1)S(1)} %broadcast_in_dim.58, bf16[8,64,4096]{2,1,0:T(8,128)(2,1)} %bitcast.46), kind=kLoop, calls=%fused_computation.11 | loop fusion | flops 4194304 | bytes 16777728 | tf_op jit(solution)/shard_map/jit(_where)/select_n | solution.py:61
  41.4 98.9 %all_to_all.26 = bf16[8,64,4096]{2,1,0:T(8,128)(2,1)} all-to-all(bf16[8,64,4096]{2,1,0:T(8,128)(2,1)} %get-tuple-element.11), channel_id=1, replica_groups=mesh['expert'=8,'hidden'=4] {'expert'}, dimensions={0} | all-to-all | bytes 8388608 | tf_op jit(solution)/shard_map/all_to_all | solution.py:63
  140.3 4.7 %all-to-all-start.2 = ((bf16[8,64,4096]{2,1,0:T(8,128)(2,1)}), bf16[8,64,4096]{2,1,0:T(8,128)(2,1)}, u32[]{:S(2)}, u32[]{:S(2)}) async-start(bf16[8,64,4096]{2,1,0:T(8,128)(2,1)} %get-tuple-element.10), calls=%async_computation.2 | async-start | bytes 8388608 | tf_op jit(solution)/shard_map/all_to_all | solution.py:64
  145.4 4.1 %fusion.6 = f32[512,256]{1,0:T(8,128)S(1)} fusion(bf16[512,4096]{1,0:T(8,128)(2,1)} %bitcast.47, bf16[1,4096,256]{2,1,0:T(8,128)(2,1)} %param.12), kind=kOutput, calls=%fused_computation.17 | convolution fusion | flops 1073741824 | bytes 6815744 | tf_op jit(solution)/shard_map/dot_general | solution.py:10
  149.5 3.3 convolution_convert_fusion.1
  152.8 84.3 %all-to-all-done.2 = bf16[8,64,4096]{2,1,0:T(8,128)(2,1)} async-done(((bf16[8,64,4096]{2,1,0:T(8,128)(2,1)}), bf16[8,64,4096]{2,1,0:T(8,128)(2,1)}, u32[]{:S(2)}, u32[]{:S(2)}) %all-to-all-start.2) | async-done | bytes 4194336 | tf_op jit(solution)/shard_map/all_to_all | solution.py:64
  237.1 3.7 fusion.14
  240.9 3.3 convolution_convert_fusion
  244.9 43.0 %reduce-scatter.3.cloned.1.call-done = bf16[512,1024]{1,0:T(8,128)(2,1)} async-done(((bf16[512,4096]{1,0:T(8,128)(2,1)}), bf16[512,1024]{1,0:T(8,128)(2,1)}) %reduce-scatter.3.cloned.1.call-update) | async-done | bytes 1048592 | tf_op jit(solution)/shard_map/reduce_scatter | solution.py:80
  287.9 5.5 %all-to-all-start.3 = ((bf16[8,64,1024]{2,1,0:T(8,128)(2,1)}), bf16[8,64,1024]{2,1,0:T(8,128)(2,1)S(1)}, u32[]{:S(2)}, u32[]{:S(2)}) async-start(bf16[8,64,1024]{2,1,0:T(8,128)(2,1)} %bitcast.50), calls=%async_computation.4 | async-start | bytes 2097152 | tf_op jit(solution)/shard_map/all_to_all | solution.py:95
  293.4 41.7 %reduce-scatter.5.cloned.1.call-done = bf16[512,1024]{1,0:T(8,128)(2,1)} async-done(((bf16[512,4096]{1,0:T(8,128)(2,1)}), bf16[512,1024]{1,0:T(8,128)(2,1)}) %reduce-scatter.5.cloned.1.call-update) | async-done | bytes 1048592 | tf_op jit(solution)/shard_map/reduce_scatter | solution.py:86
  335.1 5.5 %all-to-all-start.4 = ((bf16[8,64,1024]{2,1,0:T(8,128)(2,1)}), bf16[8,64,1024]{2,1,0:T(8,128)(2,1)}, u32[]{:S(2)}, u32[]{:S(2)}) async-start(bf16[8,64,1024]{2,1,0:T(8,128)(2,1)} %bitcast.49), calls=%async_computation.6 | async-start | bytes 2097152 | tf_op jit(solution)/shard_map/all_to_all | solution.py:102
  340.9 4.9 %fusion = bf16[1,4096,256]{2,1,0:T(8,128)(2,1)} fusion(bf16[512,4096]{1,0:T(8,128)(2,1)} %bitcast.48, bf16[512,256]{1,0:T(8,128)(2,1)S(1)} %fusion.14), kind=kOutput, calls=%fused_computation.9 | convolution fusion | flops 1074790400 | bytes 6553600 | tf_op jit(solution)/shard_map/rd,rf->df/dot_general | solution.py:27
  345.8 4.9 %fusion.1 = bf16[1,256,4096]{2,1,0:T(8,128)(2,1)} fusion(bf16[512,4096]{1,0:T(8,128)(2,1)} %bitcast.10, f32[512,256]{1,0:T(8,128)S(1)} %copy-done.4, f32[256]{0:T(256)S(1)} %bitcast.56, f32[256]{0:T(256)S(1)} %bitcast.53, f32[512]{0:T(512)S(1)} %reshape.209), kind=kOutput, calls=%fused_computation.10 | convolution fusion | flops 1075970048 | bytes 6819840 | tf_op jit(solution)/shard_map/rf,rd->fd/dot_general | solution.py:24
  352.4 3.2 gather_fusion.3
  357.2 9.3 %all-to-all-done.4 = bf16[8,64,1024]{2,1,0:T(8,128)(2,1)} async-done(((bf16[8,64,1024]{2,1,0:T(8,128)(2,1)}), bf16[8,64,1024]{2,1,0:T(8,128)(2,1)}, u32[]{:S(2)}, u32[]{:S(2)}) %all-to-all-start.4) | async-done | bytes 1048608 | tf_op jit(solution)/shard_map/all_to_all | solution.py:102
  366.5 2.8 bitcast_convert_fusion
  369.3 3.2 gather_fusion.4
  374.1 3.2 reduce_sum.44
  377.3 3.2 reduce_sum.45
  (49 shorter events, 9.6 us)
Async XLA Ops:
  7.2 142.4 %copy-start = (bf16[1,256,4096]{2,1,0:T(8,128)(2,1)S(1)}, bf16[1,256,4096]{2,1,0:T(8,128)(2,1)}, u32[]{:S(2)}) copy-start(bf16[1,256,4096]{2,1,0:T(8,128)(2,1)} %param.13) | copy-start | bytes 6291460
  7.2 14.0 %copy-start.1 = (bf16[128,4096]{1,0:T(8,128)(2,1)S(1)}, bf16[128,4096]{1,0:T(8,128)(2,1)}, u32[]{:S(2)}) copy-start(bf16[128,4096]{1,0:T(8,128)(2,1)} %param.9) | copy-start | bytes 3145732
  13.9 27.5 %all-to-all-start = ((bf16[8,1,64]{2,1,0:T(2,128)(2,1)}), bf16[8,1,64]{2,1,0:T(2,128)(2,1)S(1)}, u32[]{:S(2)}, u32[]{:S(2)}) async-start(bf16[8,1,64]{2,1,0:T(2,128)(2,1)} %convert_element_type.98), calls=%async_computation | async-start | bytes 8192 | tf_op jit(solution)/shard_map/all_to_all | solution.py:65
  140.3 4.9 %copy-start.6 = (s32[1,256]{1,0:T(1,128)S(1)}, s32[1,256]{1,0:T(1,128)}, u32[]{:S(2)}) copy-start(s32[1,256]{1,0:T(1,128)} %param.15) | copy-start | bytes 3076
  140.3 4.9 %copy-start.7 = (s32[1,256]{1,0:T(1,128)S(1)}, s32[1,256]{1,0:T(1,128)}, u32[]{:S(2)}) copy-start(s32[1,256]{1,0:T(1,128)} %param.14) | copy-start | bytes 3076
  140.3 96.8 %all-to-all-start.2 = ((bf16[8,64,4096]{2,1,0:T(8,128)(2,1)}), bf16[8,64,4096]{2,1,0:T(8,128)(2,1)}, u32[]{:S(2)}, u32[]{:S(2)}) async-start(bf16[8,64,4096]{2,1,0:T(8,128)(2,1)} %get-tuple-element.10), calls=%async_computation.2 | async-start | bytes 8388608 | tf_op jit(solution)/shard_map/all_to_all | solution.py:64
  145.0 142.9 %reduce-scatter.3.cloned.1.call-start = ((), (), s32[]{:S(2)}) async-start(), calls=%async_computation.7 | async-start | bytes 5242880 | tf_op jit(solution)/shard_map/reduce_scatter | solution.py:80
  149.5 91.3 %copy-start.3 = (f32[512,256]{1,0:T(8,128)}, f32[512,256]{1,0:T(8,128)S(1)}, u32[]{:S(2)}) copy-start(f32[512,256]{1,0:T(8,128)S(1)} %fusion.6) | copy-start | bytes 1572868
  237.1 3.7 copy-start.2
  244.2 96.5 %copy-start.5 = (s32[128,2]{0,1:T(2,128)S(1)}, s32[128,2]{0,1:T(2,128)}, u32[]{:S(2)}) copy-start(s32[128,2]{0,1:T(2,128)} %param.10) | copy-start | bytes 3076
  244.2 90.9 %reduce-scatter.5.cloned.1.call-start = ((), (), s32[]{:S(2)}) async-start(), calls=%async_computation.8 | async-start | bytes 5242880 | tf_op jit(solution)/shard_map/reduce_scatter | solution.py:86
  287.9 47.2 %all-to-all-start.3 = ((bf16[8,64,1024]{2,1,0:T(8,128)(2,1)}), bf16[8,64,1024]{2,1,0:T(8,128)(2,1)S(1)}, u32[]{:S(2)}, u32[]{:S(2)}) async-start(bf16[8,64,1024]{2,1,0:T(8,128)(2,1)} %bitcast.50), calls=%async_computation.4 | async-start | bytes 2097152 | tf_op jit(solution)/shard_map/all_to_all | solution.py:95
  335.1 31.4 %all-to-all-start.4 = ((bf16[8,64,1024]{2,1,0:T(8,128)(2,1)}), bf16[8,64,1024]{2,1,0:T(8,128)(2,1)}, u32[]{:S(2)}, u32[]{:S(2)}) async-start(bf16[8,64,1024]{2,1,0:T(8,128)(2,1)} %bitcast.49), calls=%async_computation.6 | async-start | bytes 2097152 | tf_op jit(solution)/shard_map/all_to_all | solution.py:102
  340.9 4.9 %copy-start.4 = (f32[512,256]{1,0:T(8,128)S(1)}, f32[512,256]{1,0:T(8,128)}, u32[]{:S(2)}) copy-start(f32[512,256]{1,0:T(8,128)} %copy-done.3) | copy-start | bytes 1572868
Sparse Core Ops, SparseCore 0:
  244.3 43.5 reduce-scatter.2
  290.6 44.4 reduce-scatter.4
where the time goes:
time: 388 us; the launch traced here: 387 us
  waiting for transfers between devices  179 us (46%)
  blocking collectives  98.9 us (25%)
  local copies, waits for them, and re-layouts  29.7 us (8%)
  matrix products  24.1 us (6%)
  starting transfers between devices  23.2 us (6%)
  other arithmetic  18 us (5%)
  between operations  14.3 us (4%)
    all_to_all x1, blocking collectives, shards(): lax.all_to_all(send_in, 'expert', split_axis=0, concat_axis=0, tiled=True)  98.9 us
    all_to_all x1, waiting for transfers between devices, shards(): lax.all_to_all(send_up, 'expert', split_axis=0, concat_axis=0, tiled=True)  84.3 us
    reduce_scatter x1, waiting for transfers between devices, shards(): lax.psum_scatter(kept_out.astype(jnp.float32).astype(jnp.bfloat16), 'hidd...  43 us
    reduce_scatter x1, waiting for transfers between devices, shards(): lax.psum_scatter(kept_back.astype(jnp.float32).astype(jnp.bfloat16), 'hid...  41.7 us
    gather x1, local copies, waits for them, and re-layouts, shards(): tokens[source_token]  9.95 us
    all_to_all x1, waiting for transfers between devices, shards(): lax.all_to_all(back_sum.reshape(groups, capacity, share).astype(jnp.bfloa...  9.33 us
  transfers between devices with their start and end apart: 6, of which 4 were waited for; matrix products, arithmetic and copies ran while one was open for 11% of the time, Pallas kernels for 0%

commit v1 on v0

v1 whole, which is shorter than its diff:
```python
import functools

import jax
import jax.numpy as jnp
from jax import lax
from jax.experimental import pallas as pl
from jax.experimental.pallas import tpu as pltpu
from jax.sharding import PartitionSpec as P

SHARPNESS = 2.0
LANES = 128
MESH = pl.DeviceIdType.MESH


def greet(groups, me, h, core_mate, far_mate):
    barrier = pltpu.get_barrier_semaphore()

    def hello(d, carry):
        peer = lax.rem(me + d, groups)
        pl.semaphore_signal(barrier, inc=1, device_id=(peer, h), device_id_type=MESH)
        return carry

    lax.fori_loop(1, groups, hello, 0)
    for mate in (core_mate, far_mate):
        pl.semaphore_signal(barrier, inc=1, device_id=(me, mate), device_id_type=MESH)
    pl.semaphore_wait(barrier, groups + 1)


def places():
    me = lax.axis_index("expert")
    h = lax.axis_index("hidden")
    core_mate = h + 1 - 2 * lax.rem(h, 2)
    far_mate = lax.rem(h + 2, 4)
    return me, h, core_mate, far_mate


def columns(index, width):
    return pl.ds(pl.multiple_of(index * width, width), width)


def dispatch_kernel(
    groups,
    send_in,
    send_up,
    send_gate,
    own_in,
    own_up,
    got_in,
    got_up,
    got_gate,
    far_send,
    far_recv,
    y_send,
    y_recv,
    c_send,
    c_recv,
    r_send,
    r_recv,
    own_sem,
):
    me, h, core_mate, far_mate = places()
    quarter = send_in.shape[2]
    greet(groups, me, h, core_mate, far_mate)
    mine = columns(h, quarter)
    theirs = columns(far_mate, quarter)
    tensors = ((send_in, got_in, own_in), (send_up, got_up, own_up))

    def out_copies(d):
        peer = lax.rem(me + d, groups)
        made = [
            pltpu.make_async_remote_copy(
                src_ref=src.at[peer],
                dst_ref=dst.at[me, :, mine],
                send_sem=far_send.at[t, d],
                recv_sem=far_recv.at[t, d],
                device_id=(peer, h),
                device_id_type=MESH,
            )
            for t, (src, dst, own) in enumerate(tensors)
        ]
        made.append(
            pltpu.make_async_remote_copy(
                src_ref=send_gate.at[peer],
                dst_ref=got_gate.at[me],
                send_sem=far_send.at[2, d],
                recv_sem=far_recv.at[2, d],
                device_id=(peer, h),
                device_id_type=MESH,
            )
        )
        return made

    def share(d, t, cols, mate, s_sem, r_sem):
        owner = lax.rem(me + groups - d, groups)
        block = tensors[t][1].at[owner, :, cols]
        return pltpu.make_async_remote_copy(
            src_ref=block,
            dst_ref=block,
            send_sem=s_sem.at[t, d],
            recv_sem=r_sem.at[t, d],
            device_id=(me, mate),
            device_id_type=MESH,
        )

    def begin(d, carry):
        for copy in out_copies(d):
            copy.start()
        return carry

    lax.fori_loop(1, groups, begin, 0)
    own_copies = [
        pltpu.make_async_copy(own_in, got_in.at[me], own_sem.at[0]),
        pltpu.make_async_copy(own_up, got_up.at[me], own_sem.at[1]),
        pltpu.make_async_copy(send_gate.at[me], got_gate.at[me], own_sem.at[2]),
    ]
    for copy in own_copies:
        copy.start()

    def relay(d):
        for t in range(2):
            share(d, t, mine, far_mate, y_send, y_recv).wait_recv()
            share(d, t, theirs, core_mate, r_send, r_recv).start()

    def forward(d, carry):
        arrived = out_copies(d)
        for t in range(2):
            arrived[t].wait_recv()
            share(d, t, mine, far_mate, y_send, y_recv).start()
            share(d, t, mine, core_mate, c_send, c_recv).start()

        @pl.when(d > 1)
        def _():
            relay(d - 1)

        return carry

    lax.fori_loop(1, groups, forward, 0)
    relay(groups - 1)

    def finish(d, carry):
        for copy in out_copies(d):
            copy.wait_send()
        out_copies(d)[2].wait_recv()
        for t in range(2):
            share(d, t, mine, far_mate, y_send, y_recv).wait_send()
            share(d, t, mine, core_mate, c_send, c_recv).wait()
            share(d, t, theirs, core_mate, r_send, r_recv).wait()
        return carry

    lax.fori_loop(1, groups, finish, 0)
    for copy in own_copies:
        copy.wait()


def dispatch(groups, send_in, send_up, send_gate, own_in, own_up):
    capacity, quarter = send_in.shape[1:]
    width = own_in.shape[1]
    anywhere = pl.BlockSpec(memory_space=pl.ANY)
    dma = pltpu.SemaphoreType.DMA
    return pl.pallas_call(
        functools.partial(dispatch_kernel, groups),
        out_shape=(
            jax.ShapeDtypeStruct((groups, capacity, width), jnp.bfloat16),
            jax.ShapeDtypeStruct((groups, capacity, width), jnp.bfloat16),
            jax.ShapeDtypeStruct((groups, capacity, LANES), jnp.bfloat16),
        ),
        in_specs=[anywhere] * 5,
        out_specs=(anywhere,) * 3,
        scratch_shapes=[dma((3, groups)), dma((3, groups))]
        + [dma((2, groups))] * 6
        + [dma((3,))],
        compiler_params=pltpu.CompilerParams(collective_id=0, has_side_effects=True),
    )(send_in, send_up, send_gate, own_in, own_up)


def combine_kernel(
    groups,
    part_out,
    part_back,
    home_out,
    home_back,
    core_in,
    far_out,
    far_in,
    total,
    c_send,
    c_recv,
    y_send,
    y_recv,
    far_send,
    far_recv,
):
    me, h, core_mate, far_mate = places()
    quarter = home_out.shape[2]
    parts = (part_out, part_back)
    homes = (home_out, home_back)
    greet(groups, me, h, core_mate, far_mate)
    far_core_mate = lax.rem(core_mate + 2, 4)
    mate_quarters = (core_mate, far_core_mate)

    def owner_of(d):
        return lax.rem(me + d, groups)

    def core_copy(d, t, which):
        owner = owner_of(d)
        return pltpu.make_async_remote_copy(
            src_ref=parts[t].at[owner, :, columns(mate_quarters[which], quarter)],
            dst_ref=core_in.at[t, which, owner],
            send_sem=c_send.at[t, which, d],
            recv_sem=c_recv.at[t, which, d],
            device_id=(me, core_mate),
            device_id_type=MESH,
        )

    def far_copy(d, t):
        owner = owner_of(d)
        return pltpu.make_async_remote_copy(
            src_ref=far_out.at[t, owner],
            dst_ref=far_in.at[t, owner],
            send_sem=y_send.at[t, d],
            recv_sem=y_recv.at[t, d],
            device_id=(me, far_mate),
            device_id_type=MESH,
        )

    def home_copy(d, t):
        owner = owner_of(d)
        return pltpu.make_async_remote_copy(
            src_ref=total.at[t, owner],
            dst_ref=homes[t].at[me],
            send_sem=far_send.at[t, d],
            recv_sem=far_recv.at[t, d],
            device_id=(owner, h),
            device_id_type=MESH,
        )

    def begin(i, carry):
        d = lax.rem(i + 1, groups)
        for t in range(2):
            for which in (1, 0):
                core_copy(d, t, which).start()
        return carry

    lax.fori_loop(0, groups, begin, 0)

    def first(i):
        d = lax.rem(i + 1, groups)
        owner = owner_of(d)
        for t in range(2):
            core_copy(d, t, 1).wait_recv()
            far_out[t, owner] = (
                parts[t][owner, :, columns(far_mate, quarter)].astype(jnp.float32)
                + core_in[t, 1, owner].astype(jnp.float32)
            ).astype(jnp.bfloat16)
            far_copy(d, t).start()

    def second(i, last):
        d = lax.rem(i + 1, groups)
        owner = owner_of(d)
        for t in range(2):
            core_copy(d, t, 0).wait_recv()
            far_copy(d, t).wait_recv()
            value = (
                parts[t][owner, :, columns(h, quarter)].astype(jnp.float32)
                + core_in[t, 0, owner].astype(jnp.float32)
                + far_in[t, owner].astype(jnp.float32)
            ).astype(jnp.bfloat16)
            if last:
                homes[t][owner] = value
            else:
                total[t, owner] = value
                home_copy(d, t).start()

    first(0)

    def step(i, carry):
        first(i + 1)
        second(i, False)
        return carry

    lax.fori_loop(0, groups - 1, step, 0)
    second(groups - 1, True)

    def finish(i, carry):
        d = lax.rem(i + 1, groups)
        for t in range(2):
            for which in (0, 1):
                core_copy(d, t, which).wait_send()
            far_copy(d, t).wait_send()
        return carry

    lax.fori_loop(0, groups, finish, 0)

    def close(d, carry):
        for t in range(2):
            home_copy(d, t).wait()
        return carry

    lax.fori_loop(1, groups, close, 0)


def combine(groups, part_out, part_back):
    capacity, width = part_out.shape[1:]
    quarter = width // 4
    vmem = pl.BlockSpec(memory_space=pltpu.VMEM)
    dma = pltpu.SemaphoreType.DMA
    block = (groups, capacity, quarter)
    return pl.pallas_call(
        functools.partial(combine_kernel, groups),
        out_shape=(jax.ShapeDtypeStruct(block, jnp.bfloat16),) * 2,
        in_specs=[vmem] * 2,
        out_specs=(vmem,) * 2,
        scratch_shapes=[
            pltpu.VMEM((2, 2) + block, jnp.bfloat16),
            pltpu.VMEM((2,) + block, jnp.bfloat16),
            pltpu.VMEM((2,) + block, jnp.bfloat16),
            pltpu.VMEM((2,) + block, jnp.bfloat16),
            dma((2, 2, groups)),
            dma((2, 2, groups)),
            dma((2, groups)),
            dma((2, groups)),
            dma((2, groups)),
            dma((2, groups)),
        ],
        compiler_params=pltpu.CompilerParams(
            collective_id=1, has_side_effects=True, vmem_limit_bytes=48 * 2**20
        ),
    )(part_out, part_back)


def expert_pass(inputs, upstream, weight_col, up_block, down_block, threshold_row, mask_row):
    pre = jnp.dot(inputs, up_block, preferred_element_type=jnp.float32)
    level = threshold_row.astype(jnp.float32) / 64.0
    opened = mask_row.astype(jnp.float32)
    sigma = jax.nn.sigmoid(SHARPNESS * (pre - level))
    gated = (weight_col * opened * pre * sigma).astype(jnp.bfloat16)
    back_hidden = (
        jnp.einsum("rd,fd->rf", upstream, down_block, preferred_element_type=jnp.float32)
        * weight_col
    )
    slope = opened * (sigma + SHARPNESS * pre * sigma * (1.0 - sigma))
    dpre = (back_hidden * slope).astype(jnp.bfloat16)
    part_out = jnp.dot(gated, down_block, preferred_element_type=jnp.float32)
    part_back = jnp.einsum("rf,df->rd", dpre, up_block, preferred_element_type=jnp.float32)
    grad_down = jnp.einsum("rf,rd->fd", gated, upstream, preferred_element_type=jnp.float32).astype(
        jnp.bfloat16
    )
    grad_up = jnp.einsum("rd,rf->df", inputs, dpre, preferred_element_type=jnp.float32).astype(
        jnp.bfloat16
    )
    return (part_out, part_back, grad_up, grad_down)


def shards(
    tokens, cotangent, expert_ids, gate_codes, up_weight, down_weight, threshold_state, spike_mask
):
    groups = lax.axis_size("expert")
    me = lax.axis_index("expert")
    h = lax.axis_index("hidden")
    tok_rows, width = tokens.shape
    quarter = width // lax.axis_size("hidden")
    top = expert_ids.shape[1]
    capacity = 4 * tok_rows // groups
    pairs = tok_rows * top
    slots = groups * capacity
    flat_ids = expert_ids.reshape(pairs)
    pair_index = jnp.arange(pairs, dtype=jnp.int32)
    earlier = (flat_ids[None, :] == flat_ids[:, None]) & (pair_index[None, :] < pair_index[:, None])
    place = jnp.sum(earlier.astype(jnp.int32), axis=1)
    target = (flat_ids * capacity + place).reshape(tok_rows, top)
    slot_index = jnp.arange(slots, dtype=jnp.int32)
    gates = gate_codes.astype(jnp.float32) / 256.0
    hits = [target[None, :, k] == slot_index[:, None] for k in range(top)]
    pick = functools.reduce(jnp.logical_or, hits).astype(jnp.bfloat16)
    slot_gate = sum(
        jnp.sum(jnp.where(hits[k], gates[None, :, k], 0.0), axis=1) for k in range(top)
    ).astype(jnp.bfloat16)
    send_gate = jnp.broadcast_to(slot_gate[:, None], (slots, LANES)).reshape(
        groups, capacity, LANES
    )

    def choose(which, rows):
        return jnp.dot(which, rows, preferred_element_type=jnp.float32).astype(jnp.bfloat16)

    own_pick = lax.dynamic_slice_in_dim(pick, me * capacity, capacity, 0)
    tok_cut = lax.dynamic_slice_in_dim(tokens, h * quarter, quarter, 1)
    cot_cut = lax.dynamic_slice_in_dim(cotangent, h * quarter, quarter, 1)
    got_in, got_up, got_gate = dispatch(
        groups,
        choose(pick, tok_cut).reshape(groups, capacity, quarter),
        choose(pick, cot_cut).reshape(groups, capacity, quarter),
        send_gate,
        choose(own_pick, tokens),
        choose(own_pick, cotangent),
    )
    part_out, part_back, grad_up, grad_down = expert_pass(
        got_in.reshape(slots, width),
        got_up.reshape(slots, width),
        got_gate.reshape(slots, LANES)[:, :1].astype(jnp.float32),
        up_weight[0],
        down_weight[0],
        threshold_state[0],
        spike_mask[0],
    )
    home_out, home_back = combine(
        groups,
        part_out.astype(jnp.bfloat16).reshape(groups, capacity, width),
        part_back.astype(jnp.bfloat16).reshape(groups, capacity, width),
    )

    def gather_home(home):
        return jnp.einsum(
            "st,sw->tw", pick, home.reshape(slots, quarter), preferred_element_type=jnp.float32
        ).astype(jnp.bfloat16)

    return (gather_home(home_out), gather_home(home_back), grad_up[None], grad_down[None])


def solution(mesh):
    placed = (
        P("expert", None),
        P("expert", None),
        P("expert", None),
        P("expert", None),
        P("expert", None, "hidden"),
        P("expert", "hidden", None),
        P("expert", "hidden"),
        P("expert", "hidden"),
    )
    return jax.shard_map(
        shards,
        mesh=mesh,
        in_specs=placed,
        out_specs=(
            P("expert", "hidden"),
            P("expert", "hidden"),
            P("expert", None, "hidden"),
            P("expert", "hidden", None),
        ),
        check_vma=False,
    )
```

time: 388 us -> 180 us (0.46)
  the two profiles are of different devices: /device:TPU:0 before, /device:TPU:7 now
where the time goes in v1:
time: 180 us; the launch traced here: 179 us
  Pallas kernels  143 us (79%)
  matrix products  29.1 us (16%)
  other arithmetic  4.29 us (2%)
  local copies, waits for them, and re-layouts  2.14 us (1%)
    pallas_call x1, Pallas kernels, combine(): pl.pallas_call(functools.partial(combine_kernel, groups), out_shape=(jax....  77.7 us
    pallas_call x1, Pallas kernels, dispatch(): pl.pallas_call(functools.partial(dispatch_kernel, groups), out_shape=(jax...  65.3 us
    dot_general x4, matrix products, choose(): jnp.dot(which, rows, preferred_element_type=jnp.float32)  9.45 us
    dot_general x1, matrix products, expert_pass(): pre = jnp.dot(inputs, up_block, preferred_element_type=jnp.float32)  4.26 us

profile of v1, /device:TPU:7, one launch (start us, length us, event | category | flops | bytes accessed | tf_op | source)
XLA Modules:
  0.0 179.2 jit_solution(17767827978707386183)
XLA Ops:
  0.7 0.8 convert_multiply_fusion.1
  1.5 0.7 convert_multiply_fusion
  2.2 0.7 convert_element_type.70
  2.9 0.8 copy.24
  3.8 0.2 convert_reduce_fusion
  4.0 0.1 reduce_sum.30
  4.2 0.7 multiply_add_fusion
  4.9 0.2 select_reduce_fusion
  5.3 0.8 broadcast_in_dim.46.send_gate
  6.1 2.4 %convolution_convert_fusion.4.own_up = bf16[64,4096]{1,0:T(8,128)(2,1)} fusion(bf16[128,4096]{1,0:T(8,128)(2,1)} %param.9, pred[512,128]{1,0:T(32,128)(4,1)S(1)} %fusion.19, s32[]{:T(128)S(6)} %select_n.17), kind=kOutput, calls=%fused_computation.6 | convolution fusion | flops 67371008 | bytes 1581060 | tf_op jit(solution)/shard_map/dot_general | solution.py:383
  8.4 2.4 %convolution_convert_fusion.5.own_in = bf16[64,4096]{1,0:T(8,128)(2,1)} fusion(bf16[128,4096]{1,0:T(8,128)(2,1)} %param.8, pred[512,128]{1,0:T(32,128)(4,1)S(1)} %fusion.19, s32[]{:T(128)S(6)} %select_n.17), kind=kOutput, calls=%fused_computation.7 | convolution fusion | flops 67371008 | bytes 1581060 | tf_op jit(solution)/shard_map/dot_general | solution.py:383
  10.8 2.3 %convolution_convert_fusion.7 = bf16[512,1024]{1,0:T(8,128)(2,1)} fusion(bf16[128,4096]{1,0:T(8,128)(2,1)} %param.8, s32[]{:T(128)S(6)} %select_n.14, s32[128]{0:T(128)S(1)} %get-tuple-element.17, s32[128]{0:T(128)S(1)} %get-tuple-element.16), kind=kOutput, calls=%fused_computation.15 | convolution fusion | flops 134938624 | bytes 1311748 | tf_op jit(solution)/shard_map/dot_general | solution.py:383
  13.2 2.3 %convolution_convert_fusion.6 = bf16[512,1024]{1,0:T(8,128)(2,1)} fusion(bf16[128,4096]{1,0:T(8,128)(2,1)} %param.9, s32[]{:T(128)S(6)} %select_n.14, s32[128]{0:T(128)S(1)} %get-tuple-element.17, s32[128]{0:T(128)S(1)} %get-tuple-element.16), kind=kOutput, calls=%fused_computation.14 | convolution fusion | flops 134938624 | bytes 1311748 | tf_op jit(solution)/shard_map/dot_general | solution.py:383
  15.5 65.3 %shard_map.111 = (bf16[8,64,4096]{2,1,0:T(8,128)(2,1)}, bf16[8,64,4096]{2,1,0:T(8,128)(2,1)}, bf16[8,64,128]{2,1,0:T(8,128)(2,1)}) custom-call(bf16[8,64,1024]{2,1,0:T(8,128)(2,1)} %bitcast.54, bf16[8,64,1024]{2,1,0:T(8,128)(2,1)} %bitcast.55, bf16[8,64,128]{2,1,0:T(8,128)(2,1)} %broadcast_in_dim.46.send_gate, ...), custom_call_target="tpu_custom_call" | custom-call | tf_op jit(solution)/shard_map/pallas_call | solution.py:160
  80.8 0.9 slice_convert_fusion
  81.8 4.3 %fusion.6 = f32[512,256]{1,0:T(8,128)S(1)} fusion(bf16[512,4096]{1,0:T(8,128)(2,1)} %bitcast.66, bf16[1,4096,256]{2,1,0:T(8,128)(2,1)} %param.12), kind=kOutput, calls=%fused_computation.12 | convolution fusion | flops 1073741824 | bytes 6815744 | tf_op jit(solution)/shard_map/dot_general | solution.py:332
  86.1 1.4 fusion.14
  87.5 2.8 %fusion.1 = bf16[1,256,4096]{2,1,0:T(8,128)(2,1)} fusion(bf16[512,4096]{1,0:T(8,128)(2,1)S(1)} %bitcast.69, f32[512,256]{1,0:T(8,128)S(1)} %fusion.6, f32[256]{0:T(256)S(1)} %bitcast.61, f32[256]{0:T(256)S(1)} %bitcast.64, f32[512]{0:T(512)S(1)} %bitcast.58), kind=kOutput, calls=%fused_computation.5 | convolution fusion | flops 1075970048 | bytes 6819840 | tf_op jit(solution)/shard_map/rf,rd->fd/dot_general | solution.py:345
  90.3 2.7 %fusion = bf16[1,4096,256]{2,1,0:T(8,128)(2,1)} fusion(bf16[512,4096]{1,0:T(8,128)(2,1)S(1)} %bitcast.67, bf16[512,256]{1,0:T(8,128)(2,1)S(1)} %fusion.14), kind=kOutput, calls=%fused_computation.4 | convolution fusion | flops 1074790400 | bytes 6553600 | tf_op jit(solution)/shard_map/rd,rf->df/dot_general | solution.py:348
  92.9 3.2 %convolution_convert_fusion.1 = bf16[512,4096]{1,0:T(8,128)(2,1)} fusion(bf16[1,256,4096]{2,1,0:T(8,128)(2,1)S(1)} %copy-done, f32[512,256]{1,0:T(8,128)S(1)} %fusion.6, f32[256]{0:T(256)S(1)} %bitcast.62, f32[256]{0:T(256)S(1)} %bitcast.65, f32[512]{0:T(512)S(1)} %bitcast.59), kind=kOutput, calls=%fused_computation.1 | convolution fusion | flops 1077018624 | bytes 6819840 | tf_op jit(solution)/shard_map/dot_general | solution.py:343
  96.2 3.3 %convolution_convert_fusion = bf16[512,4096]{1,0:T(8,128)(2,1)} fusion(bf16[512,256]{1,0:T(8,128)(2,1)S(1)} %fusion.14, bf16[1,4096,256]{2,1,0:T(8,128)(2,1)S(1)} %copy-done.1), kind=kOutput, calls=%fused_computation | convolution fusion | flops 1075838976 | bytes 6553600 | tf_op jit(solution)/shard_map/rf,df->rd/dot_general | solution.py:344
  99.4 77.7 %shard_map.112 = (bf16[8,64,1024]{2,1,0:T(8,128)(2,1)S(1)}, bf16[8,64,1024]{2,1,0:T(8,128)(2,1)S(1)}) custom-call(bf16[8,64,4096]{2,1,0:T(8,128)(2,1)} %bitcast.53, bf16[8,64,4096]{2,1,0:T(8,128)(2,1)} %bitcast.52), custom_call_target="tpu_custom_call" | custom-call | tf_op jit(solution)/shard_map/pallas_call | solution.py:308
  177.1 1.1 convolution_convert_fusion.9
  178.2 1.1 convolution_convert_fusion.8
  (16 shorter events, 0.5 us)
Async XLA Ops:
  0.6 85.5 %copy-start = (bf16[1,256,4096]{2,1,0:T(8,128)(2,1)S(1)}, bf16[1,256,4096]{2,1,0:T(8,128)(2,1)}, u32[]{:S(2)}) copy-start(bf16[1,256,4096]{2,1,0:T(8,128)(2,1)} %param.13) | copy-start | bytes 6291460
  81.8 4.3 %copy-start.3 = (bf16[8,64,4096]{2,1,0:T(8,128)(2,1)S(1)}, bf16[8,64,4096]{2,1,0:T(8,128)(2,1)}, u32[]{:S(2)}) copy-start(bf16[8,64,4096]{2,1,0:T(8,128)(2,1)} %get-tuple-element.11) | copy-start | bytes 12582916
  87.5 2.8 %copy-start.2 = (bf16[8,64,4096]{2,1,0:T(8,128)(2,1)S(1)}, bf16[8,64,4096]{2,1,0:T(8,128)(2,1)}, u32[]{:S(2)}) copy-start(bf16[8,64,4096]{2,1,0:T(8,128)(2,1)} %get-tuple-element.10) | copy-start | bytes 12582916
  92.9 3.3 %copy-start.1 = (bf16[1,4096,256]{2,1,0:T(8,128)(2,1)S(1)}, bf16[1,4096,256]{2,1,0:T(8,128)(2,1)}, u32[]{:S(2)}) copy-start(bf16[1,4096,256]{2,1,0:T(8,128)(2,1)} %param.12) | copy-start | bytes 6291460

commit v2 on v1

--- a/solution.py
+++ b/solution.py
@@ -328,6 +328,322 @@
     )(part_out, part_back)
 
 
+def fused_kernel(
+    groups,
+    tokens,
+    cotangent,
+    pick,
+    send_gate,
+    level,
+    opened,
+    up_any,
+    down_any,
+    home_out,
+    home_back,
+    grad_up_t,
+    grad_down,
+    got_in,
+    got_up,
+    got_gate,
+    send_buf,
+    up,
+    down,
+    gated_all,
+    dpre_all,
+    part,
+    core_in,
+    far_out,
+    far_in,
+    total,
+    w_sem,
+    far_send,
+    far_recv,
+    y_send,
+    y_recv,
+    c_send,
+    c_recv,
+    r_send,
+    r_recv,
+    back_c_send,
+    back_c_recv,
+    back_y_send,
+    back_y_recv,
+    home_send,
+    home_recv,
+):
+    me, h, core_mate, far_mate = places()
+    quarter = home_out.shape[2]
+    capacity = home_out.shape[1]
+    width = tokens.shape[1]
+    hidden_units = down.shape[0]
+    slots = groups * capacity
+    far_core_mate = lax.rem(core_mate + 2, 4)
+    mate_quarters = (core_mate, far_core_mate)
+    weight_copies = [
+        pltpu.make_async_copy(up_any, up, w_sem.at[0]),
+        pltpu.make_async_copy(down_any, down, w_sem.at[1]),
+    ]
+    for copy in weight_copies:
+        copy.start()
+    greet(groups, me, h, core_mate, far_mate)
+    mine = columns(h, quarter)
+    theirs = columns(far_mate, quarter)
+    sources = (tokens, cotangent)
+    gots = (got_in, got_up)
+    homes = (home_out, home_back)
+
+    def remote(src, dst, s_sem, r_sem, device):
+        return pltpu.make_async_remote_copy(
+            src_ref=src,
+            dst_ref=dst,
+            send_sem=s_sem,
+            recv_sem=r_sem,
+            device_id=device,
+            device_id_type=MESH,
+        )
+
+    def owner_of(d):
+        return lax.rem(me + groups - d, groups)
+
+    def out_copy(d, t):
+        peer = lax.rem(me + d, groups)
+        if t == 2:
+            src, dst = send_gate.at[peer], got_gate.at[me]
+        else:
+            src, dst = send_buf.at[t, peer], gots[t].at[me, :, mine]
+        return remote(src, dst, far_send.at[t, d], far_recv.at[t, d], (peer, h))
+
+    def share(d, t, cols, mate, s_sem, r_sem):
+        block = gots[t].at[owner_of(d), :, cols]
+        return remote(block, block, s_sem.at[t, d], r_sem.at[t, d], (me, mate))
+
+    def y_share(d, t):
+        return share(d, t, mine, far_mate, y_send, y_recv)
+
+    def core_share(d, t):
+        return share(d, t, mine, core_mate, c_send, c_recv)
+
+    def relay_share(d, t):
+        return share(d, t, theirs, core_mate, r_send, r_recv)
+
+    def core_copy(d, t, which):
+        owner = owner_of(d)
+        return remote(
+            part.at[t, owner, :, columns(mate_quarters[which], quarter)],
+            core_in.at[t, which, owner],
+            back_c_send.at[t, which, d],
+            back_c_recv.at[t, which, d],
+            (me, core_mate),
+        )
+
+    def far_copy(d, t):
+        owner = owner_of(d)
+        return remote(
+            far_out.at[t, owner],
+            far_in.at[t, owner],
+            back_y_send.at[t, d],
+            back_y_recv.at[t, d],
+            (me, far_mate),
+        )
+
+    def home_copy(d, t):
+        owner = owner_of(d)
+        return remote(
+            total.at[t, owner],
+            homes[t].at[me],
+            home_send.at[t, d],
+            home_recv.at[t, d],
+            (owner, h),
+        )
+
+    def times(a, b):
+        return jnp.dot(a, b, preferred_element_type=jnp.float32)
+
+    def times_t(a, b):
+        return lax.dot_general(a, b, (((1,), (1,)), ((), ())), preferred_element_type=jnp.float32)
+
+    def t_times(a, b):
+        return lax.dot_general(a, b, (((0,), (0,)), ((), ())), preferred_element_type=jnp.float32)
+
+    def begin(d, carry):
+        peer = lax.rem(me + d, groups)
+        for t in range(2):
+            send_buf[t, peer] = times(pick[peer], sources[t][:, mine]).astype(jnp.bfloat16)
+            out_copy(d, t).start()
+        out_copy(d, 2).start()
+        return carry
+
+    lax.fori_loop(1, groups, begin, 0)
+    for t in range(2):
+        for q in range(4):
+            cols = slice(q * quarter, (q + 1) * quarter)
+            gots[t][me, :, cols] = times(pick[me], sources[t][:, cols]).astype(jnp.bfloat16)
+    got_gate[me] = send_gate[me]
+    for copy in weight_copies:
+        copy.wait()
+
+    def forward(d):
+        for t in range(2):
+            out_copy(d, t).wait_recv()
+            y_share(d, t).start()
+            core_share(d, t).start()
+
+    def relay(d):
+        for t in range(2):
+            y_share(d, t).wait_recv()
+            relay_share(d, t).start()
+
+    def compute(d):
+        owner = owner_of(d)
+        weight_col = got_gate[owner].astype(jnp.float32)[:, :1]
+        pre = times(got_in[owner], up[...])
+        sigma = jax.nn.sigmoid(SHARPNESS * (pre - level[...]))
+        gated = (weight_col * opened[...] * pre * sigma).astype(jnp.bfloat16)
+        back_hidden = times_t(got_up[owner], down[...]) * weight_col
+        slope = opened[...] * (sigma + SHARPNESS * pre * sigma * (1.0 - sigma))
+        dpre = (back_hidden * slope).astype(jnp.bfloat16)
+        gated_all[owner] = gated
+        dpre_all[owner] = dpre
+        for q in range(4):
+            cols = slice(q * quarter, (q + 1) * quarter)
+            part[0, owner, :, cols] = times(gated, down[:, cols]).astype(jnp.bfloat16)
+            part[1, owner, :, cols] = times_t(dpre, up[cols, :]).astype(jnp.bfloat16)
+        for t in range(2):
+            for which in (1, 0):
+                core_copy(d, t, which).start()
+
+    def compute_arrived(d):
+        for t in range(2):
+            core_share(d, t).wait_recv()
+            relay_share(d, t).wait_recv()
+        out_copy(d, 2).wait_recv()
+        compute(d)
+
+    def first(d):
+        owner = owner_of(d)
+        for t in range(2):
+            core_copy(d, t, 1).wait_recv()
+            far_out[t, owner] = (
+                part[t, owner, :, theirs].astype(jnp.float32)
+                + core_in[t, 1, owner].astype(jnp.float32)
+            ).astype(jnp.bfloat16)
+            far_copy(d, t).start()
+
+    def second(d):
+        owner = owner_of(d)
+        for t in range(2):
+            core_copy(d, t, 0).wait_recv()
+            far_copy(d, t).wait_recv()
+            total[t, owner] = (
+                part[t, owner, :, mine].astype(jnp.float32)
+                + core_in[t, 0, owner].astype(jnp.float32)
+                + far_in[t, owner].astype(jnp.float32)
+            ).astype(jnp.bfloat16)
+
+            @pl.when(d > 0)
+            def _():
+                home_copy(d, t).start()
+
+    compute(0)
+
+    def step(i, carry):
+        pl.when(i < groups)(lambda: forward(i))
+        pl.when((i > 1) & (i <= groups))(lambda: relay(i - 1))
+        pl.when((i > 2) & (i <= groups + 1))(lambda: compute_arrived(i - 2))
+        pl.when(i > 2)(lambda: first(i - 3))
+        pl.when(i > 3)(lambda: second(i - 4))
+        return carry
+
+    lax.fori_loop(1, groups + 3, step, 0)
+    tile = 512
+
+    def grads(left, right, result):
+        def one(n, carry):
+            cols = columns(n, tile)
+            rows = right[:, :, cols].reshape(slots, tile)
+            result[:, cols] = t_times(left[...].reshape(slots, hidden_units), rows).astype(
+                jnp.bfloat16
+            )
+            return carry
+
+        lax.fori_loop(0, width // tile, one, 0)
+
+    grads(gated_all, got_up, grad_down)
+    second(groups - 1)
+    grads(dpre_all, got_in, grad_up_t)
+    for t in range(2):
+        homes[t][me] = total[t, me]
+
+    def finish(d, carry):
+        for t in range(2):
+            for which in (0, 1):
+                core_copy(d, t, which).wait_send()
+            far_copy(d, t).wait_send()
+
+        @pl.when(d > 0)
+        def _():
+            for t in range(2):
+                y_share(d, t).wait_send()
+                core_share(d, t).wait_send()
+                relay_share(d, t).wait_send()
+                home_copy(d, t).wait()
+            for t in range(3):
+                out_copy(d, t).wait_send()
+
+        return carry
+
+    lax.fori_loop(0, groups, finish, 0)
+
+
+def fused(groups, tokens, cotangent, pick, send_gate, level, opened, up_block, down_block):
+    capacity = pick.shape[1]
+    width = tokens.shape[1]
+    quarter = width // 4
+    hidden_units = down_block.shape[0]
+    vmem = pl.BlockSpec(memory_space=pltpu.VMEM)
+    anywhere = pl.BlockSpec(memory_space=pl.ANY)
+    dma = pltpu.SemaphoreType.DMA
+    block = (groups, capacity, quarter)
+    whole = (groups, capacity, width)
+    narrow = (groups, capacity, hidden_units)
+    half = jnp.bfloat16
+    return pl.pallas_call(
+        functools.partial(fused_kernel, groups),
+        out_shape=(
+            jax.ShapeDtypeStruct(block, half),
+            jax.ShapeDtypeStruct(block, half),
+            jax.ShapeDtypeStruct((hidden_units, width), half),
+            jax.ShapeDtypeStruct((hidden_units, width), half),
+        ),
+        in_specs=[vmem] * 6 + [anywhere] * 2,
+        out_specs=(vmem,) * 4,
+        scratch_shapes=[
+            pltpu.VMEM(whole, half),
+            pltpu.VMEM(whole, half),
+            pltpu.VMEM((groups, capacity, LANES), half),
+            pltpu.VMEM((2,) + block, half),
+            pltpu.VMEM((width, hidden_units), half),
+            pltpu.VMEM((hidden_units, width), half),
+            pltpu.VMEM(narrow, half),
+            pltpu.VMEM(narrow, half),
+            pltpu.VMEM((2,) + whole, half),
+            pltpu.VMEM((2, 2) + block, half),
+            pltpu.VMEM((2,) + block, half),
+            pltpu.VMEM((2,) + block, half),
+            pltpu.VMEM((2,) + block, half),
+            dma((2,)),
+            dma((3, groups)),
+            dma((3, groups)),
+        ]
+        + [dma((2, groups))] * 6
+        + [dma((2, 2, groups))] * 2
+        + [dma((2, groups))] * 4,
+        compiler_params=pltpu.CompilerParams(
+            collective_id=2, has_side_effects=True, vmem_limit_bytes=58 * 2**20
+        ),
+    )(tokens, cotangent, pick, send_gate, level, opened, up_block, down_block)
+
+
 def expert_pass(inputs, upstream, weight_col, up_block, down_block, threshold_row, mask_row):
     pre = jnp.dot(inputs, up_block, preferred_element_type=jnp.float32)
     level = threshold_row.astype(jnp.float32) / 64.0
@@ -382,31 +698,45 @@
     def choose(which, rows):
         return jnp.dot(which, rows, preferred_element_type=jnp.float32).astype(jnp.bfloat16)
 
-    own_pick = lax.dynamic_slice_in_dim(pick, me * capacity, capacity, 0)
-    tok_cut = lax.dynamic_slice_in_dim(tokens, h * quarter, quarter, 1)
-    cot_cut = lax.dynamic_slice_in_dim(cotangent, h * quarter, quarter, 1)
-    got_in, got_up, got_gate = dispatch(
-        groups,
-        choose(pick, tok_cut).reshape(groups, capacity, quarter),
-        choose(pick, cot_cut).reshape(groups, capacity, quarter),
-        send_gate,
-        choose(own_pick, tokens),
-        choose(own_pick, cotangent),
-    )
-    part_out, part_back, grad_up, grad_down = expert_pass(
-        got_in.reshape(slots, width),
-        got_up.reshape(slots, width),
-        got_gate.reshape(slots, LANES)[:, :1].astype(jnp.float32),
-        up_weight[0],
-        down_weight[0],
-        threshold_state[0],
-        spike_mask[0],
-    )
-    home_out, home_back = combine(
-        groups,
-        part_out.astype(jnp.bfloat16).reshape(groups, capacity, width),
-        part_back.astype(jnp.bfloat16).reshape(groups, capacity, width),
-    )
+    if capacity % 16 == 0:
+        home_out, home_back, grad_up_t, grad_down = fused(
+            groups,
+            tokens,
+            cotangent,
+            pick.reshape(groups, capacity, tok_rows),
+            send_gate,
+            threshold_state.astype(jnp.float32) / 64.0,
+            spike_mask.astype(jnp.float32),
+            up_weight[0],
+            down_weight[0],
+        )
+        grad_up = grad_up_t.T
+    else:
+        own_pick = lax.dynamic_slice_in_dim(pick, me * capacity, capacity, 0)
+        tok_cut = lax.dynamic_slice_in_dim(tokens, h * quarter, quarter, 1)
+        cot_cut = lax.dynamic_slice_in_dim(cotangent, h * quarter, quarter, 1)
+        got_in, got_up, got_gate = dispatch(
+            groups,
+            choose(pick, tok_cut).reshape(groups, capacity, quarter),
+            choose(pick, cot_cut).reshape(groups, capacity, quarter),
+            send_gate,
+            choose(own_pick, tokens),
+            choose(own_pick, cotangent),
+        )
+        part_out, part_back, grad_up, grad_down = expert_pass(
+            got_in.reshape(slots, width),
+            got_up.reshape(slots, width),
+            got_gate.reshape(slots, LANES)[:, :1].astype(jnp.float32),
+            up_weight[0],
+            down_weight[0],
+            threshold_state[0],
+            spike_mask[0],
+        )
+        home_out, home_back = combine(
+            groups,
+            part_out.astype(jnp.bfloat16).reshape(groups, capacity, width),
+            part_back.astype(jnp.bfloat16).reshape(groups, capacity, width),
+        )
 
     def gather_home(home):
         return jnp.einsum(

time: 180 us -> 149 us (0.83)
  the two profiles are of different devices: /device:TPU:7 before, /device:TPU:0 now
where the time goes in v2:
time: 149 us; the launch traced here: 148 us
  Pallas kernels  130 us (87%)
  local copies, waits for them, and re-layouts  7.55 us (5%)
  other arithmetic  5.09 us (3%)
  matrix products  4.57 us (3%)
    pallas_call x1, Pallas kernels, fused(): pl.pallas_call(functools.partial(fused_kernel, groups), out_shape=(jax.Sh...  130 us
    unnamed x5, local copies, waits for them, and re-layouts  6.32 us
    dot_general x2, matrix products, gather_home(): jnp.einsum('st,sw->tw', pick, home.reshape(slots, quarter), preferred_ele...  4.57 us

profile of v2, /device:TPU:0, one launch (start us, length us, event | category | flops | bytes accessed | tf_op | source)
XLA Modules:
  0.0 148.3 jit_solution(15983893045962217594)
XLA Ops:
  0.6 0.7 convert_multiply_fusion.1
  1.3 1.2 convert_multiply_fusion.level
  2.6 1.2 convert_element_type.38.opened
  3.8 0.8 copy.25
  4.6 0.1 eq.69
  4.7 0.2 convert_reduce_fusion
  4.9 0.1 reduce_sum.30
  5.1 0.1 copy.26
  5.1 0.7 multiply_add_fusion.1
  5.8 0.2 select_reduce_fusion
  6.1 0.1 convert_element_type.36
  6.2 0.8 or_convert_fusion.pick
  7.0 0.8 broadcast_in_dim.43.send_gate
  7.7 130.4 %shard_map.111 = (bf16[8,64,1024]{2,1,0:T(8,128)(2,1)}, bf16[8,64,1024]{2,1,0:T(8,128)(2,1)}, bf16[256,4096]{1,0:T(8,128)(2,1)}, bf16[256,4096]{1,0:T(8,128)(2,1)}) custom-call(bf16[128,4096]{1,0:T(8,128)(2,1)} %tokens.1, bf16[128,4096]{1,0:T(8,128)(2,1)} %cotangent.1, bf16[8,64,128]{2,1,0:T(8,128)(2,1)} %or_convert_fusion.pick, ...), custom_call_target="tpu_custom_call" | custom-call | tf_op jit(solution)/shard_map/pallas_call | solution.py:610
  138.1 2.3 %convolution_convert_fusion.1 = bf16[128,1024]{1,0:T(8,128)(2,1)} fusion(bf16[512,1024]{1,0:T(8,128)(2,1)} %bitcast.23, s32[128]{0:T(128)S(1)} %get-tuple-element.35, s32[128]{0:T(128)S(1)} %get-tuple-element.34), kind=kOutput, calls=%fused_computation.1 | convolution fusion | flops 134545408 | bytes 1311744 | tf_op jit(solution)/shard_map/st,sw->tw/dot_general | solution.py:742
  140.4 2.3 %convolution_convert_fusion = bf16[128,1024]{1,0:T(8,128)(2,1)} fusion(bf16[512,1024]{1,0:T(8,128)(2,1)} %bitcast.22, s32[128]{0:T(128)S(1)} %get-tuple-element.35, s32[128]{0:T(128)S(1)} %get-tuple-element.34), kind=kOutput, calls=%fused_computation | convolution fusion | flops 134545408 | bytes 1311744 | tf_op jit(solution)/shard_map/st,sw->tw/dot_general | solution.py:742
  142.7 0.0 copy-start
  142.7 4.2 %copy.27 = bf16[1,4096,256]{2,1,0:T(8,128)(2,1)} copy(bf16[1,4096,256]{1,2,0:T(8,128)(2,1)} %bitcast.21) | data formatting | bytes 4194304
  146.9 0.0 copy-done
  146.9 1.3 copy.29
  (4 shorter events, 0.0 us)
Async XLA Ops:
  142.7 4.2 %copy-start = (bf16[256,4096]{1,0:T(8,128)(2,1)S(1)}, bf16[256,4096]{1,0:T(8,128)(2,1)}, u32[]{:S(2)}) copy-start(bf16[256,4096]{1,0:T(8,128)(2,1)} %get-tuple-element.11) | copy-start | bytes 6291460

commit v3 on v2

--- a/solution.py
+++ b/solution.py
@@ -332,16 +332,23 @@
     groups,
     tokens,
     cotangent,
-    pick,
+    target_col,
+    target_row,
+    code_row,
+    threshold,
+    mask,
+    up_any,
+    down_any,
+    layer_out,
+    token_grad,
+    grad_up,
+    grad_down,
+    home_out,
+    home_back,
     send_gate,
     level,
     opened,
-    up_any,
-    down_any,
-    home_out,
-    home_back,
-    grad_up_t,
-    grad_down,
+    cross_buf,
     got_in,
     got_up,
     got_gate,
@@ -388,6 +395,8 @@
     greet(groups, me, h, core_mate, far_mate)
     mine = columns(h, quarter)
     theirs = columns(far_mate, quarter)
+    level[...] = threshold[...].astype(jnp.float32) / 64.0
+    opened[...] = mask[...].astype(jnp.float32)
     sources = (tokens, cotangent)
     gots = (got_in, got_up)
     homes = (home_out, home_back)
@@ -402,11 +411,33 @@
             device_id_type=MESH,
         )
 
+    def partner(d):
+        total_bits, bit = 0, 1
+        while bit < groups:
+            total_bits = total_bits + lax.rem(me // bit + d // bit, 2) * bit
+            bit *= 2
+        return total_bits
+
     def owner_of(d):
-        return lax.rem(me + groups - d, groups)
+        return partner(d)
+
+    def turn(i):
+        return lax.rem(3 * i, groups)
+
+    def select(peer):
+        rows = lax.broadcasted_iota(jnp.int32, (capacity, tokens.shape[0]), 0) + peer * capacity
+        hits = [rows == target_row[k : k + 1, :] for k in range(target_row.shape[0])]
+        gate = 0.0
+        chosen = 0.0
+        for k, hit in enumerate(hits):
+            value = code_row[k : k + 1, :].astype(jnp.float32) / 256.0
+            gate = gate + jnp.sum(jnp.where(hit, value, 0.0), axis=1, keepdims=True)
+            chosen = chosen + jnp.where(hit, 1.0, 0.0)
+        spread = jnp.broadcast_to(gate, (capacity, LANES)).astype(jnp.bfloat16)
+        return chosen.astype(jnp.bfloat16), spread
 
     def out_copy(d, t):
-        peer = lax.rem(me + d, groups)
+        peer = partner(d)
         if t == 2:
             src, dst = send_gate.at[peer], got_gate.at[me]
         else:
@@ -419,6 +450,15 @@
 
     def y_share(d, t):
         return share(d, t, mine, far_mate, y_send, y_recv)
+
+    def cross_copy(t):
+        return remote(
+            cross_buf.at[t],
+            gots[t].at[me, :, theirs],
+            y_send.at[t, 1],
+            y_recv.at[t, 1],
+            (partner(1), h),
+        )
 
     def core_share(d, t):
         return share(d, t, mine, core_mate, c_send, c_recv)
@@ -465,32 +505,44 @@
     def t_times(a, b):
         return lax.dot_general(a, b, (((0,), (0,)), ((), ())), preferred_element_type=jnp.float32)
 
-    def begin(d, carry):
-        peer = lax.rem(me + d, groups)
-        for t in range(2):
-            send_buf[t, peer] = times(pick[peer], sources[t][:, mine]).astype(jnp.bfloat16)
+    def begin(i, carry):
+        d = turn(i)
+        peer = partner(d)
+        chosen, spread = select(peer)
+        send_gate[peer] = spread
+        for t in range(2):
+            send_buf[t, peer] = times(chosen, sources[t][:, mine]).astype(jnp.bfloat16)
             out_copy(d, t).start()
         out_copy(d, 2).start()
+
+        @pl.when(d == 1)
+        def _():
+            for t in range(2):
+                cross_buf[t] = times(chosen, sources[t][:, theirs]).astype(jnp.bfloat16)
+                cross_copy(t).start()
+
         return carry
 
     lax.fori_loop(1, groups, begin, 0)
+    own_chosen, own_spread = select(me)
     for t in range(2):
         for q in range(4):
             cols = slice(q * quarter, (q + 1) * quarter)
-            gots[t][me, :, cols] = times(pick[me], sources[t][:, cols]).astype(jnp.bfloat16)
-    got_gate[me] = send_gate[me]
+            gots[t][me, :, cols] = times(own_chosen, sources[t][:, cols]).astype(jnp.bfloat16)
+    got_gate[me] = own_spread
     for copy in weight_copies:
         copy.wait()
 
     def forward(d):
         for t in range(2):
             out_copy(d, t).wait_recv()
-            y_share(d, t).start()
+            pl.when(d != 1)(lambda: y_share(d, t).start())
             core_share(d, t).start()
 
     def relay(d):
         for t in range(2):
-            y_share(d, t).wait_recv()
+            pl.when(d != 1)(lambda: y_share(d, t).wait_recv())
+            pl.when(d == 1)(lambda: cross_copy(t).wait_recv())
             relay_share(d, t).start()
 
     def compute(d):
@@ -547,30 +599,33 @@
     compute(0)
 
     def step(i, carry):
-        pl.when(i < groups)(lambda: forward(i))
-        pl.when((i > 1) & (i <= groups))(lambda: relay(i - 1))
-        pl.when((i > 2) & (i <= groups + 1))(lambda: compute_arrived(i - 2))
-        pl.when(i > 2)(lambda: first(i - 3))
-        pl.when(i > 3)(lambda: second(i - 4))
+        pl.when(i < groups)(lambda: forward(turn(i)))
+        pl.when(i == 1)(lambda: first(0))
+        pl.when((i > 1) & (i <= groups))(lambda: relay(turn(i - 1)))
+        pl.when(i > 3)(lambda: first(turn(i - 3)))
+        pl.when(i > 3)(lambda: second(turn(i - 4)))
+        pl.when((i > 2) & (i <= groups + 1))(lambda: compute_arrived(turn(i - 2)))
         return carry
 
     lax.fori_loop(1, groups + 3, step, 0)
     tile = 512
 
-    def grads(left, right, result):
+    def grads(left, right, result, turned):
         def one(n, carry):
             cols = columns(n, tile)
             rows = right[:, :, cols].reshape(slots, tile)
-            result[:, cols] = t_times(left[...].reshape(slots, hidden_units), rows).astype(
-                jnp.bfloat16
-            )
+            value = t_times(left[...].reshape(slots, hidden_units), rows)
+            if turned:
+                result[cols, :] = value.T.astype(jnp.bfloat16)
+            else:
+                result[:, cols] = value.astype(jnp.bfloat16)
             return carry
 
         lax.fori_loop(0, width // tile, one, 0)
 
-    grads(gated_all, got_up, grad_down)
-    second(groups - 1)
-    grads(dpre_all, got_in, grad_up_t)
+    grads(gated_all, got_up, grad_down, False)
+    second(turn(groups - 1))
+    grads(dpre_all, got_in, grad_up, True)
     for t in range(2):
         homes[t][me] = total[t, me]
 
@@ -583,7 +638,8 @@
         @pl.when(d > 0)
         def _():
             for t in range(2):
-                y_share(d, t).wait_send()
+                pl.when(d != 1)(lambda: y_share(d, t).wait_send())
+                pl.when(d == 1)(lambda: cross_copy(t).wait_send())
                 core_share(d, t).wait_send()
                 relay_share(d, t).wait_send()
                 home_copy(d, t).wait()
@@ -593,10 +649,16 @@
         return carry
 
     lax.fori_loop(0, groups, finish, 0)
-
-
-def fused(groups, tokens, cotangent, pick, send_gate, level, opened, up_block, down_block):
-    capacity = pick.shape[1]
+    lanes = lax.broadcasted_iota(jnp.int32, (tokens.shape[0], slots), 1)
+    gather = 0.0
+    for k in range(target_col.shape[1]):
+        gather = gather + jnp.where(lanes == target_col[:, k : k + 1], 1.0, 0.0)
+    gather = gather.astype(jnp.bfloat16)
+    for home, result in ((home_out, layer_out), (home_back, token_grad)):
+        result[...] = times(gather, home[...].reshape(slots, quarter)).astype(jnp.bfloat16)
+
+
+def fused(groups, capacity, tokens, cotangent, target, codes, threshold, mask, up_block, down_block):
     width = tokens.shape[1]
     quarter = width // 4
     hidden_units = down_block.shape[0]
@@ -610,14 +672,20 @@
     return pl.pallas_call(
         functools.partial(fused_kernel, groups),
         out_shape=(
-            jax.ShapeDtypeStruct(block, half),
-            jax.ShapeDtypeStruct(block, half),
-            jax.ShapeDtypeStruct((hidden_units, width), half),
+            jax.ShapeDtypeStruct((tokens.shape[0], quarter), half),
+            jax.ShapeDtypeStruct((tokens.shape[0], quarter), half),
+            jax.ShapeDtypeStruct((width, hidden_units), half),
             jax.ShapeDtypeStruct((hidden_units, width), half),
         ),
-        in_specs=[vmem] * 6 + [anywhere] * 2,
+        in_specs=[vmem] * 7 + [anywhere] * 2,
         out_specs=(vmem,) * 4,
         scratch_shapes=[
+            pltpu.VMEM(block, half),
+            pltpu.VMEM(block, half),
+            pltpu.VMEM((groups, capacity, LANES), half),
+            pltpu.VMEM((1, hidden_units), jnp.float32),
+            pltpu.VMEM((1, hidden_units), jnp.float32),
+            pltpu.VMEM((2, capacity, quarter), half),
             pltpu.VMEM(whole, half),
             pltpu.VMEM(whole, half),
             pltpu.VMEM((groups, capacity, LANES), half),
@@ -641,7 +709,7 @@
         compiler_params=pltpu.CompilerParams(
             collective_id=2, has_side_effects=True, vmem_limit_bytes=58 * 2**20
         ),
-    )(tokens, cotangent, pick, send_gate, level, opened, up_block, down_block)
+    )(tokens, cotangent, target, target.T, codes.T, threshold, mask, up_block, down_block)
 
 
 def expert_pass(inputs, upstream, weight_col, up_block, down_block, threshold_row, mask_row):
@@ -684,6 +752,20 @@
     earlier = (flat_ids[None, :] == flat_ids[:, None]) & (pair_index[None, :] < pair_index[:, None])
     place = jnp.sum(earlier.astype(jnp.int32), axis=1)
     target = (flat_ids * capacity + place).reshape(tok_rows, top)
+    if capacity % 16 == 0 and groups & (groups - 1) == 0:
+        layer_out, token_grad, grad_up, grad_down = fused(
+            groups,
+            capacity,
+            tokens,
+            cotangent,
+            target,
+            gate_codes,
+            threshold_state,
+            spike_mask,
+            up_weight[0],
+            down_weight[0],
+        )
+        return (layer_out, token_grad, grad_up[None], grad_down[None])
     slot_index = jnp.arange(slots, dtype=jnp.int32)
     gates = gate_codes.astype(jnp.float32) / 256.0
     hits = [target[None, :, k] == slot_index[:, None] for k in range(top)]
@@ -698,45 +780,31 @@
     def choose(which, rows):
         return jnp.dot(which, rows, preferred_element_type=jnp.float32).astype(jnp.bfloat16)
 
-    if capacity % 16 == 0:
-        home_out, home_back, grad_up_t, grad_down = fused(
-            groups,
-            tokens,
-            cotangent,
-            pick.reshape(groups, capacity, tok_rows),
-            send_gate,
-            threshold_state.astype(jnp.float32) / 64.0,
-            spike_mask.astype(jnp.float32),
-            up_weight[0],
-            down_weight[0],
-        )
-        grad_up = grad_up_t.T
-    else:
-        own_pick = lax.dynamic_slice_in_dim(pick, me * capacity, capacity, 0)
-        tok_cut = lax.dynamic_slice_in_dim(tokens, h * quarter, quarter, 1)
-        cot_cut = lax.dynamic_slice_in_dim(cotangent, h * quarter, quarter, 1)
-        got_in, got_up, got_gate = dispatch(
-            groups,
-            choose(pick, tok_cut).reshape(groups, capacity, quarter),
-            choose(pick, cot_cut).reshape(groups, capacity, quarter),
-            send_gate,
-            choose(own_pick, tokens),
-            choose(own_pick, cotangent),
-        )
-        part_out, part_back, grad_up, grad_down = expert_pass(
-            got_in.reshape(slots, width),
-            got_up.reshape(slots, width),
-            got_gate.reshape(slots, LANES)[:, :1].astype(jnp.float32),
-            up_weight[0],
-            down_weight[0],
-            threshold_state[0],
-            spike_mask[0],
-        )
-        home_out, home_back = combine(
-            groups,
-            part_out.astype(jnp.bfloat16).reshape(groups, capacity, width),
-            part_back.astype(jnp.bfloat16).reshape(groups, capacity, width),
-        )
+    own_pick = lax.dynamic_slice_in_dim(pick, me * capacity, capacity, 0)
+    tok_cut = lax.dynamic_slice_in_dim(tokens, h * quarter, quarter, 1)
+    cot_cut = lax.dynamic_slice_in_dim(cotangent, h * quarter, quarter, 1)
+    got_in, got_up, got_gate = dispatch(
+        groups,
+        choose(pick, tok_cut).reshape(groups, capacity, quarter),
+        choose(pick, cot_cut).reshape(groups, capacity, quarter),
+        send_gate,
+        choose(own_pick, tokens),
+        choose(own_pick, cotangent),
+    )
+    part_out, part_back, grad_up, grad_down = expert_pass(
+        got_in.reshape(slots, width),
+        got_up.reshape(slots, width),
+        got_gate.reshape(slots, LANES)[:, :1].astype(jnp.float32),
+        up_weight[0],
+        down_weight[0],
+        threshold_state[0],
+        spike_mask[0],
+    )
+    home_out, home_back = combine(
+        groups,
+        part_out.astype(jnp.bfloat16).reshape(groups, capacity, width),
+        part_back.astype(jnp.bfloat16).reshape(groups, capacity, width),
+    )
 
     def gather_home(home):
         return jnp.einsum(

time: 149 us -> 133 us (0.89)
  Pallas kernels: 130 us -> 122 us
  matrix products: 4.57 us -> 0 us
  other arithmetic: 5.09 us -> 0.89 us
  local copies, waits for them, and re-layouts: 7.55 us -> 9.73 us
    pallas_call x1, Pallas kernels: 130 us -> 122 us  [fused(): pl.pallas_call(functools.partial(fused_kernel, groups), out_shape=(jax.Sh...]
    dot_general x2 -> x0, matrix products: 4.57 us -> none  [gather_home(): jnp.einsum('st,sw->tw', pick, home.reshape(slots, quarter), preferred_ele...]
    unnamed x5 -> x9, local copies, waits for them, and re-layouts: 6.32 us -> 8.65 us
    convert_element_type x3 -> x0, other arithmetic: 2.05 us -> none  [the longest x1 1.24 us: shards(): spike_mask.astype(jnp.float32)]
    div x2 -> x0, other arithmetic: 1.93 us -> none  [the longest x1 1.24 us: shards(): threshold_state.astype(jnp.float32) / 64.0]
where the time goes in v3:
time: 133 us
  Pallas kernels  122 us (92%)
  local copies, waits for them, and re-layouts  9.73 us (7%)
    pallas_call x1, Pallas kernels, fused(): pl.pallas_call(functools.partial(fused_kernel, groups), out_shape=(jax.Sh...  122 us
    unnamed x9, local copies, waits for them, and re-layouts  8.65 us

profile of v3, /device:TPU:0, one launch (start us, length us, event | category | flops | bytes accessed | tf_op | source)
XLA Modules:
  0.0 132.8 jit_solution(11014912443346921028)
XLA Ops:
  0.6 0.8 copy.16
  1.4 0.1 eq.15
  1.6 0.2 convert_reduce_fusion
  1.7 0.1 reduce_sum.12
  1.9 0.1 copy.17
  2.0 0.7 multiply_add_fusion
  2.7 0.0 copy-start.1
  2.7 0.7 copy.18.target_col
  3.4 0.0 copy-done.1
  3.4 121.6 %shard_map.111 = (bf16[128,1024]{1,0:T(8,128)(2,1)}, bf16[128,1024]{1,0:T(8,128)(2,1)}, bf16[4096,256]{1,0:T(8,128)(2,1)}, bf16[256,4096]{1,0:T(8,128)(2,1)}) custom-call(bf16[128,4096]{1,0:T(8,128)(2,1)} %tokens.1, bf16[128,4096]{1,0:T(8,128)(2,1)} %cotangent.1, s32[128,2]{1,0:T(8,128)} %copy.18.target_col, s32[2,128]{1,0:T(2,128)} %bitcast.10, ...), custom_call_target="tpu_custom_call" | custom-call | tf_op jit(solution)/shard_map/pallas_call | solution.py:672
  125.0 1.7 %copy.23 = bf16[128,1024]{1,0:T(8,128)(2,1)} copy(bf16[128,1024]{1,0:T(8,128)(2,1)} %get-tuple-element.16) | data formatting | bytes 524288
  126.6 1.7 %copy.24 = bf16[128,1024]{1,0:T(8,128)(2,1)} copy(bf16[128,1024]{1,0:T(8,128)(2,1)} %get-tuple-element.17) | data formatting | bytes 524288
  128.3 0.0 copy-start
  128.3 3.2 %copy.25 = bf16[1,4096,256]{2,1,0:T(8,128)(2,1)} copy(bf16[1,4096,256]{2,1,0:T(8,128)(2,1)} %bitcast.7) | data formatting | bytes 4194304
  131.5 0.0 copy-done
  131.5 1.3 copy.26
Async XLA Ops:
  2.7 0.7 copy-start.1
  128.3 3.2 %copy-start = (bf16[256,4096]{1,0:T(8,128)(2,1)S(1)}, bf16[256,4096]{1,0:T(8,128)(2,1)}, u32[]{:S(2)}) copy-start(bf16[256,4096]{1,0:T(8,128)(2,1)} %get-tuple-element.11) | copy-start | bytes 6291460

commit v4 on v3

--- a/solution.py
+++ b/solution.py
@@ -422,7 +422,7 @@
         return partner(d)
 
     def turn(i):
-        return lax.rem(3 * i, groups)
+        return lax.rem(5 * i, groups)
 
     def select(peer):
         rows = lax.broadcasted_iota(jnp.int32, (capacity, tokens.shape[0]), 0) + peer * capacity
@@ -656,6 +656,29 @@
     gather = gather.astype(jnp.bfloat16)
     for home, result in ((home_out, layer_out), (home_back, token_grad)):
         result[...] = times(gather, home[...].reshape(slots, quarter)).astype(jnp.bfloat16)
+
+
+def write_kernel(*refs):
+    half = (len(refs) - 1) // 2
+    sems = refs[-1]
+    copies = [
+        pltpu.make_async_copy(refs[i], refs[half + i], sems.at[i]) for i in range(half)
+    ]
+    for copy in copies:
+        copy.start()
+    for copy in copies:
+        copy.wait()
+
+
+def write_out(results):
+    anywhere = pl.BlockSpec(memory_space=pl.ANY)
+    return pl.pallas_call(
+        write_kernel,
+        out_shape=tuple(jax.ShapeDtypeStruct(r.shape, r.dtype) for r in results),
+        in_specs=[anywhere] * len(results),
+        out_specs=(anywhere,) * len(results),
+        scratch_shapes=[pltpu.SemaphoreType.DMA((len(results),))],
+    )(*results)
 
 
 def fused(groups, capacity, tokens, cotangent, target, codes, threshold, mask, up_block, down_block):
@@ -753,7 +776,7 @@
     place = jnp.sum(earlier.astype(jnp.int32), axis=1)
     target = (flat_ids * capacity + place).reshape(tok_rows, top)
     if capacity % 16 == 0 and groups & (groups - 1) == 0:
-        layer_out, token_grad, grad_up, grad_down = fused(
+        results = fused(
             groups,
             capacity,
             tokens,
@@ -765,6 +788,7 @@
             up_weight[0],
             down_weight[0],
         )
+        layer_out, token_grad, grad_up, grad_down = write_out(results)
         return (layer_out, token_grad, grad_up[None], grad_down[None])
     slot_index = jnp.arange(slots, dtype=jnp.int32)
     gates = gate_codes.astype(jnp.float32) / 256.0

time: 133 us -> 269 us (2.02)
  Pallas kernels: 122 us -> 265 us
  local copies, waits for them, and re-layouts: 9.73 us -> 1.87 us
    pallas_call x0 -> x1, Pallas kernels: none -> 144 us  [write_out(): pl.pallas_call(write_kernel, out_shape=tuple((jax.ShapeDtypeStruct(r.shap...]
    unnamed x9 -> x3, local copies, waits for them, and re-layouts: 8.65 us -> 0.79 us
where the time goes in v4:
time: 269 us
  Pallas kernels  265 us (99%)
    pallas_call x1, Pallas kernels, write_out(): pl.pallas_call(write_kernel, out_shape=tuple((jax.ShapeDtypeStruct(r.shap...  144 us
    pallas_call x1, Pallas kernels, fused(): pl.pallas_call(functools.partial(fused_kernel, groups), out_shape=(jax.Sh...  121 us

profile of v4, /device:TPU:0, one launch (start us, length us, event | category | flops | bytes accessed | tf_op | source)
XLA Modules:
  0.0 268.6 jit_solution(598793822489219004)
XLA Ops:
  0.6 0.8 copy.16
  1.4 0.1 eq.15
  1.6 0.2 convert_reduce_fusion
  1.7 0.1 reduce_sum.12
  1.9 0.1 copy.17
  2.0 0.7 multiply_add_fusion
  2.7 0.0 copy-start
  2.7 0.7 copy.18.target_col
  3.4 0.0 copy-done
  3.4 121.1 %shard_map.111 = (bf16[128,1024]{1,0:T(8,128)(2,1)}, bf16[128,1024]{1,0:T(8,128)(2,1)}, bf16[4096,256]{1,0:T(8,128)(2,1)}, bf16[256,4096]{1,0:T(8,128)(2,1)}) custom-call(bf16[128,4096]{1,0:T(8,128)(2,1)} %tokens.1, bf16[128,4096]{1,0:T(8,128)(2,1)} %cotangent.1, s32[128,2]{1,0:T(8,128)} %copy.18.target_col, s32[2,128]{1,0:T(2,128)} %bitcast.8, ...), custom_call_target="tpu_custom_call" | custom-call | tf_op jit(solution)/shard_map/pallas_call | solution.py:695
  124.6 144.1 %shard_map.112 = (bf16[128,1024]{1,0:T(8,128)(2,1)}, bf16[128,1024]{1,0:T(8,128)(2,1)}, bf16[4096,256]{1,0:T(8,128)(2,1)}, bf16[256,4096]{1,0:T(8,128)(2,1)}) custom-call(bf16[128,1024]{1,0:T(8,128)(2,1)} %get-tuple-element.12.refs_0_, bf16[128,1024]{1,0:T(8,128)(2,1)} %get-tuple-element.13.refs_1_, bf16[4096,256]{1,0:T(8,128)(2,1)} %get-tuple-element.14.refs_2_, ...), custom_call_target="tpu_custom_call" | custom-call | tf_op jit(solution)/shard_map/pallas_call | solution.py:675
Async XLA Ops:
  2.7 0.7 copy-start

commit v5 on v4

--- a/solution.py
+++ b/solution.py
@@ -659,15 +659,18 @@
 
 
 def write_kernel(*refs):
-    half = (len(refs) - 1) // 2
-    sems = refs[-1]
-    copies = [
-        pltpu.make_async_copy(refs[i], refs[half + i], sems.at[i]) for i in range(half)
-    ]
-    for copy in copies:
-        copy.start()
-    for copy in copies:
-        copy.wait()
+    count = (len(refs) - 2) // 3
+    sources, results, held = refs[:count], refs[count : 2 * count], refs[2 * count : 3 * count]
+    in_sems, out_sems = refs[3 * count :]
+    loads = [pltpu.make_async_copy(sources[i], held[i], in_sems.at[i]) for i in range(count)]
+    stores = [pltpu.make_async_copy(held[i], results[i], out_sems.at[i]) for i in range(count)]
+    for load in loads:
+        load.start()
+    for load, store in zip(loads, stores):
+        load.wait()
+        store.start()
+    for store in stores:
+        store.wait()
 
 
 def write_out(results):
@@ -677,7 +680,9 @@
         out_shape=tuple(jax.ShapeDtypeStruct(r.shape, r.dtype) for r in results),
         in_specs=[anywhere] * len(results),
         out_specs=(anywhere,) * len(results),
-        scratch_shapes=[pltpu.SemaphoreType.DMA((len(results),))],
+        scratch_shapes=[pltpu.VMEM(r.shape, r.dtype) for r in results]
+        + [pltpu.SemaphoreType.DMA((len(results),))] * 2,
+        compiler_params=pltpu.CompilerParams(vmem_limit_bytes=24 * 2**20),
     )(*results)
 
 

time: 269 us -> 132 us (0.49)
  Pallas kernels: 265 us -> 124 us
  local copies, waits for them, and re-layouts: 1.87 us -> 6.95 us
    pallas_call x1, Pallas kernels: 144 us -> 2.57 us  [write_out(): pl.pallas_call(write_kernel, out_shape=tuple((jax.ShapeDtypeStruct(r.shap...]
    unnamed x3 -> x11, local copies, waits for them, and re-layouts: 0.79 us -> 5.86 us
where the time goes in v5:
time: 132 us
  Pallas kernels  124 us (94%)
  local copies, waits for them, and re-layouts  6.95 us (5%)
    pallas_call x1, Pallas kernels, fused(): pl.pallas_call(functools.partial(fused_kernel, groups), out_shape=(jax.Sh...  121 us
    unnamed x11, local copies, waits for them, and re-layouts  5.86 us

profile of v5, /device:TPU:0, one launch (start us, length us, event | category | flops | bytes accessed | tf_op | source)
XLA Modules:
  0.0 132.2 jit_solution(16258081434043012899)
XLA Ops:
  0.6 0.8 copy.16
  1.4 0.1 eq.15
  1.6 0.2 convert_reduce_fusion
  1.7 0.1 reduce_sum.12
  1.9 0.1 copy.17
  2.0 0.7 multiply_add_fusion
  2.7 0.0 copy-start.4
  2.7 0.7 copy.18.target_col
  3.4 0.0 copy-done.4
  3.4 121.1 %shard_map.111 = (bf16[128,1024]{1,0:T(8,128)(2,1)}, bf16[128,1024]{1,0:T(8,128)(2,1)}, bf16[4096,256]{1,0:T(8,128)(2,1)}, bf16[256,4096]{1,0:T(8,128)(2,1)}) custom-call(bf16[128,4096]{1,0:T(8,128)(2,1)} %tokens.1, bf16[128,4096]{1,0:T(8,128)(2,1)} %cotangent.1, s32[128,2]{1,0:T(8,128)} %copy.18.target_col, s32[2,128]{1,0:T(2,128)} %bitcast.8, ...), custom_call_target="tpu_custom_call" | custom-call | tf_op jit(solution)/shard_map/pallas_call | solution.py:700
  124.5 0.0 copy-start
  124.5 1.6 %copy-done = bf16[4096,256]{1,0:T(8,128)(2,1)S(1)} copy-done((bf16[4096,256]{1,0:T(8,128)(2,1)S(1)}, bf16[4096,256]{1,0:T(8,128)(2,1)}, u32[]{:S(2)}) %copy-start) | copy-done | bytes 2097176
  126.1 0.0 copy-start.1
  126.1 1.6 %copy-done.1 = bf16[256,4096]{1,0:T(8,128)(2,1)S(1)} copy-done((bf16[256,4096]{1,0:T(8,128)(2,1)S(1)}, bf16[256,4096]{1,0:T(8,128)(2,1)}, u32[]{:S(2)}) %copy-start.1) | copy-done | bytes 2097176
  127.7 0.0 copy-start.2
  127.7 0.9 copy-done.2
  128.7 0.0 copy-start.3
  128.7 0.9 copy-done.3
  129.6 2.6 %shard_map.112 = (bf16[128,1024]{1,0:T(8,128)(2,1)}, bf16[128,1024]{1,0:T(8,128)(2,1)}, bf16[4096,256]{1,0:T(8,128)(2,1)}, bf16[256,4096]{1,0:T(8,128)(2,1)}) custom-call(bf16[128,1024]{1,0:T(8,128)(2,1)S(1)} %copy-done.2, bf16[128,1024]{1,0:T(8,128)(2,1)S(1)} %copy-done.3, bf16[4096,256]{1,0:T(8,128)(2,1)S(1)} %copy-done, bf16[256,4096]{1,0:T(8,128)(2,1)S(1)} %copy-done.1), custom_call_target="tpu_custom_call" | custom-call | tf_op jit(solution)/shard_map/pallas_call | solution.py:678
Async XLA Ops:
  2.7 0.7 copy-start.4
  124.5 1.6 %copy-start = (bf16[4096,256]{1,0:T(8,128)(2,1)S(1)}, bf16[4096,256]{1,0:T(8,128)(2,1)}, u32[]{:S(2)}) copy-start(bf16[4096,256]{1,0:T(8,128)(2,1)} %get-tuple-element.14.refs_2_) | copy-start | bytes 6291460
  126.1 1.6 %copy-start.1 = (bf16[256,4096]{1,0:T(8,128)(2,1)S(1)}, bf16[256,4096]{1,0:T(8,128)(2,1)}, u32[]{:S(2)}) copy-start(bf16[256,4096]{1,0:T(8,128)(2,1)} %get-tuple-element.15.refs_3_) | copy-start | bytes 6291460
  127.7 0.9 copy-start.2
  128.7 0.9 copy-start.3
